TPU v7x, 32 devices: a whole 2x2x4 slice. The times are simulated.
32 devices in a mesh: grp: 2 (over y), col: 4 (over z), seq: 4 (over x, core).
Axes of the slice: x: 2, y: 2, z: 4, core: 2. Of those that a mesh axis runs over, the one named last changes fastest.
Arguments:
- row_query: bfloat16 [256, 16, 768], P(('grp', 'seq'), 'col'), parts along dimension 0, may hold values from -6 to 6
- row_key: bfloat16 [256, 16, 768], P(('grp', 'seq'), 'col'), parts along dimension 0, may hold values from -6 to 6
- row_value: bfloat16 [256, 16, 768], P(('grp', 'seq'), 'col'), parts along dimension 0, may hold values from -6 to 6
- row_grad: bfloat16 [256, 16, 768], P(('grp', 'seq'), 'col'), parts along dimension 0, may hold values from -48 to 48
- col_query: bfloat16 [256, 16, 768], P(('grp', 'seq'), 'col'), parts along dimension 0, may hold values from -11 to 11
- col_key: bfloat16 [256, 16, 768], P(('grp', 'seq'), 'col'), parts along dimension 0, may hold values from -11 to 11
- col_value: bfloat16 [256, 16, 768], P(('grp', 'seq'), 'col'), parts along dimension 0, may hold values from -6 to 6
- col_grad: bfloat16 [256, 16, 768], P(('grp', 'seq'), 'col'), parts along dimension 0, may hold values from -48 to 48
Outputs:
- row_dquery: bfloat16 [256, 16, 768], P(('grp', 'seq'), 'col'), parts along dimension 0
- row_dkey: bfloat16 [256, 16, 768], P(('grp', 'seq'), 'col'), parts along dimension 0
- row_dvalue: bfloat16 [256, 16, 768], P(('grp', 'seq'), 'col'), parts along dimension 0
- col_dquery: bfloat16 [256, 16, 768], P(('grp', 'seq'), 'col'), parts along dimension 0
- col_dkey: bfloat16 [256, 16, 768], P(('grp', 'seq'), 'col'), parts along dimension 0
- col_dvalue: bfloat16 [256, 16, 768], P(('grp', 'seq'), 'col'), parts along dimension 0
There are 2 independent parts, one for each index of `grp`. A program takes and returns all parts, laid end to end along the dimension named above; each array names one. Nothing has to cross between parts.
All inputs are finite; a program needn't handle non-finite values.
Results may differ from a plain program's by a relative error of at most 0.009.
Values may be sent and summed in bfloat16 or wider, within the bound.
No kernel may reach another device: no remote copies, remote signals or barrier semaphores. Data moves between devices by JAX's collectives and lax.ppermute only.
A program may use at most 64 MiB of HBM per device.

v0:
```python
import jax
import jax.numpy as jnp
from jax import lax
from jax.sharding import PartitionSpec as P

HEADS = 12
HEAD = 64


def tied_terms(scores, prob_grad, row_scale):
    row_probs = jax.nn.softmax(scores, axis=-1)
    row_delta = jnp.sum(row_probs * prob_grad, axis=-1, keepdims=True)
    score_gradient_part = row_probs * (prob_grad - row_delta) * row_scale
    return (row_probs.astype(jnp.bfloat16), score_gradient_part.astype(jnp.bfloat16))


def split_heads(block):
    return block.reshape(block.shape[0], block.shape[1] // HEAD, HEAD)


def column_core(query_row_block, key_row_block, value_row_block, gradient_row_block, col_scale):
    scores = (
        jnp.einsum(
            "qzd,izd->zqi", query_row_block, key_row_block, preferred_element_type=jnp.float32
        )
        * col_scale
    )
    prob_grad = jnp.einsum(
        "qzd,izd->zqi", gradient_row_block, value_row_block, preferred_element_type=jnp.float32
    )
    col_probs = jax.nn.softmax(scores, axis=-1)
    col_delta = jnp.sum(col_probs * prob_grad, axis=-1, keepdims=True)
    score_gradient_part = (col_probs * (prob_grad - col_delta) * col_scale).astype(jnp.bfloat16)
    attention_weight_rows = col_probs.astype(jnp.bfloat16)
    query_grad = jnp.einsum(
        "qvc,cqb->vqb", score_gradient_part, key_row_block, preferred_element_type=jnp.float32
    )
    key_gradient_part = jnp.einsum(
        "wzc,zwi->cwi", score_gradient_part, query_row_block, preferred_element_type=jnp.float32
    )
    value_gradient_part = jnp.einsum(
        "wzc,zwi->cwi",
        attention_weight_rows,
        gradient_row_block,
        preferred_element_type=jnp.float32,
    )
    return (
        query_grad.astype(jnp.bfloat16),
        key_gradient_part.astype(jnp.bfloat16),
        value_gradient_part.astype(jnp.bfloat16),
    )


def local(row_query, row_key, row_value, row_grad, col_query, col_key, col_value, col_grad):
    seq_dev, col_dev, width = row_query.shape
    seqs = seq_dev * lax.axis_size("seq")
    cols = col_dev * lax.axis_size("col")
    row_scale = HEAD ** (-0.5) * seqs ** (-0.5)
    col_scale = HEAD ** (-0.5)
    moved = (
        lax.all_to_all(row_query, "col", split_axis=0, concat_axis=1, tiled=True),
        lax.all_to_all(row_key, "col", split_axis=0, concat_axis=1, tiled=True),
        lax.all_to_all(row_value, "col", split_axis=0, concat_axis=1, tiled=True),
        lax.all_to_all(row_grad, "col", split_axis=0, concat_axis=1, tiled=True),
    )
    own_rows = moved[0].shape[0]
    shape_four = (own_rows, cols, HEADS, HEAD)
    query_row_block = moved[0].reshape(shape_four)
    key_row_block = moved[1].reshape(shape_four)
    value_row_block = moved[2].reshape(shape_four)
    gradient_row_block = moved[3].reshape(shape_four)
    score_part = (
        jnp.einsum(
            "sihe,sjhe->hij", query_row_block, key_row_block, preferred_element_type=jnp.float32
        )
        * row_scale
    )
    prob_part = jnp.einsum(
        "sihe,sjhe->hij", gradient_row_block, value_row_block, preferred_element_type=jnp.float32
    )
    scores, prob_grad = lax.psum((score_part, prob_part), ("col", "seq"))
    attention_weight_rows, score_gradient_part = tied_terms(scores, prob_grad, row_scale)
    query_grad = jnp.einsum(
        "hij,sjhe->sihe", score_gradient_part, key_row_block, preferred_element_type=jnp.float32
    )
    key_gradient_part = jnp.einsum(
        "hij,sihe->sjhe", score_gradient_part, query_row_block, preferred_element_type=jnp.float32
    )
    value_gradient_part = jnp.einsum(
        "hij,sihe->sjhe",
        attention_weight_rows,
        gradient_row_block,
        preferred_element_type=jnp.float32,
    )
    row_back = (
        lax.all_to_all(
            query_grad.astype(jnp.bfloat16).reshape(own_rows, cols, width),
            "col",
            split_axis=1,
            concat_axis=0,
            tiled=True,
        ),
        lax.all_to_all(
            key_gradient_part.astype(jnp.bfloat16).reshape(own_rows, cols, width),
            "col",
            split_axis=1,
            concat_axis=0,
            tiled=True,
        ),
        lax.all_to_all(
            value_gradient_part.astype(jnp.bfloat16).reshape(own_rows, cols, width),
            "col",
            split_axis=1,
            concat_axis=0,
            tiled=True,
        ),
    )
    flat_width = col_dev * width
    col_moved = (
        lax.all_to_all(
            col_query.reshape(seq_dev, flat_width), "seq", split_axis=1, concat_axis=0, tiled=True
        ),
        lax.all_to_all(
            col_key.reshape(seq_dev, flat_width), "seq", split_axis=1, concat_axis=0, tiled=True
        ),
        lax.all_to_all(
            col_value.reshape(seq_dev, flat_width), "seq", split_axis=1, concat_axis=0, tiled=True
        ),
        lax.all_to_all(
            col_grad.reshape(seq_dev, flat_width), "seq", split_axis=1, concat_axis=0, tiled=True
        ),
    )
    col_grads = column_core(
        split_heads(col_moved[0]),
        split_heads(col_moved[1]),
        split_heads(col_moved[2]),
        split_heads(col_moved[3]),
        col_scale,
    )
    share_width = col_moved[0].shape[1]
    col_back = (
        lax.all_to_all(
            col_grads[0].reshape(seqs, share_width), "seq", split_axis=0, concat_axis=1, tiled=True
        ),
        lax.all_to_all(
            col_grads[1].reshape(seqs, share_width), "seq", split_axis=0, concat_axis=1, tiled=True
        ),
        lax.all_to_all(
            col_grads[2].reshape(seqs, share_width), "seq", split_axis=0, concat_axis=1, tiled=True
        ),
    )
    return (
        row_back[0],
        row_back[1],
        row_back[2],
        col_back[0].reshape(seq_dev, col_dev, width),
        col_back[1].reshape(seq_dev, col_dev, width),
        col_back[2].reshape(seq_dev, col_dev, width),
    )


def solution(mesh):
    in_specs = (
        P(("grp", "seq"), "col", None),
        P(("grp", "seq"), "col", None),
        P(("grp", "seq"), "col", None),
        P(("grp", "seq"), "col", None),
        P(("grp", "seq"), "col", None),
        P(("grp", "seq"), "col", None),
        P(("grp", "seq"), "col", None),
        P(("grp", "seq"), "col", None),
    )
    out_specs = (
        P(("grp", "seq"), "col", None),
        P(("grp", "seq"), "col", None),
        P(("grp", "seq"), "col", None),
        P(("grp", "seq"), "col", None),
        P(("grp", "seq"), "col", None),
        P(("grp", "seq"), "col", None),
    )
    return jax.shard_map(local, mesh=mesh, in_specs=in_specs, out_specs=out_specs, check_vma=False)
```

profile of v0, /device:TPU:0, one launch (start us, length us, event | category | flops | bytes accessed | tf_op | source)
XLA Modules:
  0.0 195.9 jit_solution(17410516336404553708)
XLA Ops:
  0.6 1.6 copy.133
  2.3 4.3 %all-to-all-start.8 = ((bf16[32,4,768]{2,0,1:T(8,128)(2,1)}), bf16[32,4,768]{2,0,1:T(8,128)(2,1)S(1)}, u32[]{:S(2)}, u32[]{:S(2)}) async-start(bf16[32,4,768]{2,0,1:T(8,128)(2,1)} %copy.133), calls=%async_computation.8 | async-start | bytes 393216 | tf_op jit(solution)/shard_map/all_to_all | solution.py:123
  6.6 0.7 copy.136
  7.3 4.6 %all-to-all-done.8 = bf16[32,4,768]{2,0,1:T(8,128)(2,1)S(1)} async-done(((bf16[32,4,768]{2,0,1:T(8,128)(2,1)}), bf16[32,4,768]{2,0,1:T(8,128)(2,1)S(1)}, u32[]{:S(2)}, u32[]{:S(2)}) %all-to-all-start.8) | async-done | bytes 196640 | tf_op jit(solution)/shard_map/all_to_all | solution.py:123
  11.9 3.4 %all-to-all-start.9 = ((bf16[32,4,768]{2,0,1:T(8,128)(2,1)}), bf16[32,4,768]{2,0,1:T(8,128)(2,1)S(1)}, u32[]{:S(2)}, u32[]{:S(2)}) async-start(bf16[32,4,768]{2,0,1:T(8,128)(2,1)} %copy.136), calls=%async_computation.9 | async-start | bytes 393216 | tf_op jit(solution)/shard_map/all_to_all | solution.py:129
  15.3 0.7 copy.137
  16.0 4.6 %all-to-all-done.9 = bf16[32,4,768]{2,0,1:T(8,128)(2,1)S(1)} async-done(((bf16[32,4,768]{2,0,1:T(8,128)(2,1)}), bf16[32,4,768]{2,0,1:T(8,128)(2,1)S(1)}, u32[]{:S(2)}, u32[]{:S(2)}) %all-to-all-start.9) | async-done | bytes 196640 | tf_op jit(solution)/shard_map/all_to_all | solution.py:129
  20.6 3.4 %all-to-all-start.10 = ((bf16[32,4,768]{2,0,1:T(8,128)(2,1)}), bf16[32,4,768]{2,0,1:T(8,128)(2,1)S(1)}, u32[]{:S(2)}, u32[]{:S(2)}) async-start(bf16[32,4,768]{2,0,1:T(8,128)(2,1)} %copy.137), calls=%async_computation.10 | async-start | bytes 393216 | tf_op jit(solution)/shard_map/all_to_all | solution.py:126
  24.0 5.2 %all-to-all-done.10 = bf16[32,4,768]{2,0,1:T(8,128)(2,1)S(1)} async-done(((bf16[32,4,768]{2,0,1:T(8,128)(2,1)}), bf16[32,4,768]{2,0,1:T(8,128)(2,1)S(1)}, u32[]{:S(2)}, u32[]{:S(2)}) %all-to-all-start.10) | async-done | bytes 196640 | tf_op jit(solution)/shard_map/all_to_all | solution.py:126
  29.3 7.7 %all_to_all.214 = bf16[32,4,768]{2,0,1:T(8,128)(2,1)S(1)} all-to-all(bf16[32,4,768]{2,0,1:T(8,128)(2,1)S(1)} %copy.132), channel_id=1, replica_groups=mesh['grp'=2,'col'=4,'seq'=4] {'seq'}, dimensions={1} | all-to-all | bytes 393216 | tf_op jit(solution)/shard_map/all_to_all | solution.py:120
  37.0 12.7 %all_to_all.215 = bf16[32,4,768]{2,1,0:T(4,128)(2,1)S(1)} all-to-all(bf16[32,4,768]{2,1,0:T(4,128)(2,1)S(1)} %copy-done.3), channel_id=1, replica_groups=mesh['grp'=2,'col'=4,'seq'=4] {'col'}, dimensions={0} | all-to-all | bytes 393216 | tf_op jit(solution)/shard_map/all_to_all | solution.py:63
  49.7 3.4 %all-to-all-start.2 = ((bf16[32,4,768]{2,1,0:T(4,128)(2,1)}), bf16[32,4,768]{2,1,0:T(4,128)(2,1)S(1)}, u32[]{:S(2)}, u32[]{:S(2)}) async-start(bf16[32,4,768]{2,1,0:T(4,128)(2,1)} %param.11), calls=%async_computation.2 | async-start | bytes 393216 | tf_op jit(solution)/shard_map/all_to_all | solution.py:64
  53.1 0.3 reshape.108
  53.4 0.4 copy.135
  53.8 0.3 reshape.109
  54.1 0.4 copy.138
  54.5 0.3 reshape.110
  54.8 0.3 reshape.107
  55.2 0.4 copy.134
  55.8 3.5 %all-to-all-done.2 = bf16[32,4,768]{2,1,0:T(4,128)(2,1)S(1)} async-done(((bf16[32,4,768]{2,1,0:T(4,128)(2,1)}), bf16[32,4,768]{2,1,0:T(4,128)(2,1)S(1)}, u32[]{:S(2)}, u32[]{:S(2)}) %all-to-all-start.2) | async-done | bytes 196640 | tf_op jit(solution)/shard_map/all_to_all | solution.py:64
  59.4 3.4 %all-to-all-start.1 = ((bf16[32,4,768]{2,1,0:T(4,128)(2,1)}), bf16[32,4,768]{2,1,0:T(4,128)(2,1)S(1)}, u32[]{:S(2)}, u32[]{:S(2)}) async-start(bf16[32,4,768]{2,1,0:T(4,128)(2,1)} %param.9), calls=%async_computation.1 | async-start | bytes 393216 | tf_op jit(solution)/shard_map/all_to_all | solution.py:62
  62.7 0.4 fusion.59
  63.2 0.3 fusion.15
  63.5 5.4 %all-to-all-done.1 = bf16[32,4,768]{2,1,0:T(4,128)(2,1)S(1)} async-done(((bf16[32,4,768]{2,1,0:T(4,128)(2,1)}), bf16[32,4,768]{2,1,0:T(4,128)(2,1)S(1)}, u32[]{:S(2)}, u32[]{:S(2)}) %all-to-all-start.1) | async-done | bytes 196640 | tf_op jit(solution)/shard_map/all_to_all | solution.py:62
  68.9 3.4 %all-to-all-start = ((bf16[32,4,768]{2,1,0:T(4,128)(2,1)}), bf16[32,4,768]{2,1,0:T(4,128)(2,1)S(1)}, u32[]{:S(2)}, u32[]{:S(2)}) async-start(bf16[32,4,768]{2,1,0:T(4,128)(2,1)} %param.8), calls=%async_computation | async-start | bytes 393216 | tf_op jit(solution)/shard_map/all_to_all | solution.py:61
  72.3 0.4 fusion.13
  72.7 0.4 copy.142
  73.1 1.0 all_to_all.191
  74.1 0.4 copy.145
  74.6 1.0 all_to_all.194
  75.5 0.6 fusion.14
  76.2 0.4 copy.148
  76.6 1.0 all_to_all.197
  77.6 0.3 reshape.103
  78.0 0.3 reshape.102
  78.4 0.3 reshape.101
  78.7 3.4 %all-to-all-start.11 = ((bf16[4,32,768]{2,1,0:T(8,128)(2,1)}), bf16[4,32,768]{2,1,0:T(8,128)(2,1)S(1)}, u32[]{:S(2)}, u32[]{:S(2)}) async-start(bf16[4,32,768]{2,1,0:T(8,128)(2,1)} %all_to_all.191), calls=%async_computation.11 | async-start | bytes 393216 | tf_op jit(solution)/shard_map/all_to_all | solution.py:142
  82.1 0.3 reshape.100
  82.5 0.5 fusion.21
  83.0 0.5 convolution_bitcast_fusion
  83.5 64.1 %all-reduce = (f32[12,16,16]{2,1,0:T(8,128)S(1)}, f32[12,16,16]{2,1,0:T(8,128)S(1)}) all-reduce(f32[12,16,16]{2,1,0:T(8,128)S(1)} %convolution_bitcast_fusion, f32[12,16,16]{2,1,0:T(8,128)S(1)} %fusion.21), channel_id=1, replica_groups=mesh['grp'=2,'col'=4,'seq'=4] {'col','seq'}, use_global_device_ids=true, to_apply=%region_3.0 | all-reduce | flops 6144 | bytes 49152 | tf_op jit(solution)/shard_map/psum | solution.py:81
  147.6 3.4 %all-to-all-start.12 = ((bf16[4,32,768]{2,1,0:T(8,128)(2,1)}), bf16[4,32,768]{2,1,0:T(8,128)(2,1)S(1)}, u32[]{:S(2)}, u32[]{:S(2)}) async-start(bf16[4,32,768]{2,1,0:T(8,128)(2,1)} %all_to_all.194), calls=%async_computation.12 | async-start | bytes 393216 | tf_op jit(solution)/shard_map/all_to_all | solution.py:145
  151.0 1.9 fusion.58
  152.9 3.4 %all-to-all-done.12 = bf16[4,32,768]{2,1,0:T(8,128)(2,1)S(1)} async-done(((bf16[4,32,768]{2,1,0:T(8,128)(2,1)}), bf16[4,32,768]{2,1,0:T(8,128)(2,1)S(1)}, u32[]{:S(2)}, u32[]{:S(2)}) %all-to-all-start.12) | async-done | bytes 196640 | tf_op jit(solution)/shard_map/all_to_all | solution.py:145
  156.3 3.4 %all-to-all-start.13 = ((bf16[4,32,768]{2,1,0:T(8,128)(2,1)}), bf16[4,32,768]{2,1,0:T(8,128)(2,1)S(1)}, u32[]{:S(2)}, u32[]{:S(2)}) async-start(bf16[4,32,768]{2,1,0:T(8,128)(2,1)} %all_to_all.197), calls=%async_computation.13 | async-start | bytes 393216 | tf_op jit(solution)/shard_map/all_to_all | solution.py:148
  159.7 0.7 fusion.10
  160.7 1.0 reshape.116
  161.7 3.3 %all-to-all-done.13 = bf16[4,32,768]{2,1,0:T(8,128)(2,1)S(1)} async-done(((bf16[4,32,768]{2,1,0:T(8,128)(2,1)}), bf16[4,32,768]{2,1,0:T(8,128)(2,1)S(1)}, u32[]{:S(2)}, u32[]{:S(2)}) %all-to-all-start.13) | async-done | bytes 196640 | tf_op jit(solution)/shard_map/all_to_all | solution.py:148
  165.0 3.5 %all-to-all-start.4 = ((bf16[8,16,768]{2,0,1:T(8,128)(2,1)}), bf16[8,16,768]{2,0,1:T(8,128)(2,1)S(1)}, u32[]{:S(2)}, u32[]{:S(2)}) async-start(bf16[8,16,768]{2,0,1:T(8,128)(2,1)} %reshape.116), calls=%async_computation.4 | async-start | bytes 393216 | tf_op jit(solution)/shard_map/all_to_all | solution.py:96
  168.5 0.8 fusion.11
  169.6 1.0 reshape.117
  170.6 5.3 %all-to-all-done.4 = bf16[8,16,768]{2,0,1:T(8,128)(2,1)S(1)} async-done(((bf16[8,16,768]{2,0,1:T(8,128)(2,1)}), bf16[8,16,768]{2,0,1:T(8,128)(2,1)S(1)}, u32[]{:S(2)}, u32[]{:S(2)}) %all-to-all-start.4) | async-done | bytes 196640 | tf_op jit(solution)/shard_map/all_to_all | solution.py:96
  175.9 3.4 %all-to-all-start.5 = ((bf16[8,16,768]{2,0,1:T(8,128)(2,1)}), bf16[8,16,768]{2,0,1:T(8,128)(2,1)S(1)}, u32[]{:S(2)}, u32[]{:S(2)}) async-start(bf16[8,16,768]{2,0,1:T(8,128)(2,1)} %reshape.117), calls=%async_computation.5 | async-start | bytes 393216 | tf_op jit(solution)/shard_map/all_to_all | solution.py:103
  179.3 0.7 fusion.12
  180.3 1.0 reshape.118
  181.3 4.2 %all-to-all-done.5 = bf16[8,16,768]{2,0,1:T(8,128)(2,1)S(1)} async-done(((bf16[8,16,768]{2,0,1:T(8,128)(2,1)}), bf16[8,16,768]{2,0,1:T(8,128)(2,1)S(1)}, u32[]{:S(2)}, u32[]{:S(2)}) %all-to-all-start.5) | async-done | bytes 196640 | tf_op jit(solution)/shard_map/all_to_all | solution.py:103
  185.5 3.4 %all-to-all-start.6 = ((bf16[8,16,768]{2,0,1:T(8,128)(2,1)}), bf16[8,16,768]{2,0,1:T(8,128)(2,1)S(1)}, u32[]{:S(2)}, u32[]{:S(2)}) async-start(bf16[8,16,768]{2,0,1:T(8,128)(2,1)} %reshape.118), calls=%async_computation.6 | async-start | bytes 393216 | tf_op jit(solution)/shard_map/all_to_all | solution.py:110
  188.9 0.8 copy.152
  189.7 0.8 copy.153
  190.5 0.8 copy.154
  191.4 0.8 copy.149
  192.2 0.8 copy.150
  193.1 2.0 %all-to-all-done.6 = bf16[8,16,768]{2,0,1:T(8,128)(2,1)S(1)} async-done(((bf16[8,16,768]{2,0,1:T(8,128)(2,1)}), bf16[8,16,768]{2,0,1:T(8,128)(2,1)S(1)}, u32[]{:S(2)}, u32[]{:S(2)}) %all-to-all-start.6) | async-done | bytes 196640 | tf_op jit(solution)/shard_map/all_to_all | solution.py:110
  195.1 0.8 copy.151
  (22 shorter events, 1.3 us)
Async XLA Ops:
  2.3 4.3 %copy-start = (bf16[32,4,768]{2,1,0:T(4,128)(2,1)S(1)}, bf16[32,4,768]{2,1,0:T(4,128)(2,1)}, u32[]{:S(2)}) copy-start(bf16[32,4,768]{2,1,0:T(4,128)(2,1)} %param.15) | copy-start | bytes 589828
  2.3 9.7 %all-to-all-start.8 = ((bf16[32,4,768]{2,0,1:T(8,128)(2,1)}), bf16[32,4,768]{2,0,1:T(8,128)(2,1)S(1)}, u32[]{:S(2)}, u32[]{:S(2)}) async-start(bf16[32,4,768]{2,0,1:T(8,128)(2,1)} %copy.133), calls=%async_computation.8 | async-start | bytes 393216 | tf_op jit(solution)/shard_map/all_to_all | solution.py:123
  7.3 8.0 %copy-start.1 = (bf16[32,4,768]{2,1,0:T(4,128)(2,1)S(1)}, bf16[32,4,768]{2,1,0:T(4,128)(2,1)}, u32[]{:S(2)}) copy-start(bf16[32,4,768]{2,1,0:T(4,128)(2,1)} %param.14) | copy-start | bytes 589828
  11.9 8.7 %all-to-all-start.9 = ((bf16[32,4,768]{2,0,1:T(8,128)(2,1)}), bf16[32,4,768]{2,0,1:T(8,128)(2,1)S(1)}, u32[]{:S(2)}, u32[]{:S(2)}) async-start(bf16[32,4,768]{2,0,1:T(8,128)(2,1)} %copy.136), calls=%async_computation.9 | async-start | bytes 393216 | tf_op jit(solution)/shard_map/all_to_all | solution.py:129
  16.0 8.0 %copy-start.2 = (bf16[32,4,768]{2,1,0:T(4,128)(2,1)S(1)}, bf16[32,4,768]{2,1,0:T(4,128)(2,1)}, u32[]{:S(2)}) copy-start(bf16[32,4,768]{2,1,0:T(4,128)(2,1)} %param.12) | copy-start | bytes 589828
  20.6 8.7 %all-to-all-start.10 = ((bf16[32,4,768]{2,0,1:T(8,128)(2,1)}), bf16[32,4,768]{2,0,1:T(8,128)(2,1)S(1)}, u32[]{:S(2)}, u32[]{:S(2)}) async-start(bf16[32,4,768]{2,0,1:T(8,128)(2,1)} %copy.137), calls=%async_computation.10 | async-start | bytes 393216 | tf_op jit(solution)/shard_map/all_to_all | solution.py:126
  24.0 13.0 %copy-start.3 = (bf16[32,4,768]{2,1,0:T(4,128)(2,1)S(1)}, bf16[32,4,768]{2,1,0:T(4,128)(2,1)}, u32[]{:S(2)}) copy-start(bf16[32,4,768]{2,1,0:T(4,128)(2,1)} %param.10) | copy-start | bytes 589828
  49.7 9.7 %all-to-all-start.2 = ((bf16[32,4,768]{2,1,0:T(4,128)(2,1)}), bf16[32,4,768]{2,1,0:T(4,128)(2,1)S(1)}, u32[]{:S(2)}, u32[]{:S(2)}) async-start(bf16[32,4,768]{2,1,0:T(4,128)(2,1)} %param.11), calls=%async_computation.2 | async-start | bytes 393216 | tf_op jit(solution)/shard_map/all_to_all | solution.py:64
  59.4 9.6 %all-to-all-start.1 = ((bf16[32,4,768]{2,1,0:T(4,128)(2,1)}), bf16[32,4,768]{2,1,0:T(4,128)(2,1)S(1)}, u32[]{:S(2)}, u32[]{:S(2)}) async-start(bf16[32,4,768]{2,1,0:T(4,128)(2,1)} %param.9), calls=%async_computation.1 | async-start | bytes 393216 | tf_op jit(solution)/shard_map/all_to_all | solution.py:62
  68.9 9.8 %all-to-all-start = ((bf16[32,4,768]{2,1,0:T(4,128)(2,1)}), bf16[32,4,768]{2,1,0:T(4,128)(2,1)S(1)}, u32[]{:S(2)}, u32[]{:S(2)}) async-start(bf16[32,4,768]{2,1,0:T(4,128)(2,1)} %param.8), calls=%async_computation | async-start | bytes 393216 | tf_op jit(solution)/shard_map/all_to_all | solution.py:61
  78.7 68.9 %all-to-all-start.11 = ((bf16[4,32,768]{2,1,0:T(8,128)(2,1)}), bf16[4,32,768]{2,1,0:T(8,128)(2,1)S(1)}, u32[]{:S(2)}, u32[]{:S(2)}) async-start(bf16[4,32,768]{2,1,0:T(8,128)(2,1)} %all_to_all.191), calls=%async_computation.11 | async-start | bytes 393216 | tf_op jit(solution)/shard_map/all_to_all | solution.py:142
  147.6 8.7 %all-to-all-start.12 = ((bf16[4,32,768]{2,1,0:T(8,128)(2,1)}), bf16[4,32,768]{2,1,0:T(8,128)(2,1)S(1)}, u32[]{:S(2)}, u32[]{:S(2)}) async-start(bf16[4,32,768]{2,1,0:T(8,128)(2,1)} %all_to_all.194), calls=%async_computation.12 | async-start | bytes 393216 | tf_op jit(solution)/shard_map/all_to_all | solution.py:145
  156.3 8.7 %all-to-all-start.13 = ((bf16[4,32,768]{2,1,0:T(8,128)(2,1)}), bf16[4,32,768]{2,1,0:T(8,128)(2,1)S(1)}, u32[]{:S(2)}, u32[]{:S(2)}) async-start(bf16[4,32,768]{2,1,0:T(8,128)(2,1)} %all_to_all.197), calls=%async_computation.13 | async-start | bytes 393216 | tf_op jit(solution)/shard_map/all_to_all | solution.py:148
  165.0 10.9 %all-to-all-start.4 = ((bf16[8,16,768]{2,0,1:T(8,128)(2,1)}), bf16[8,16,768]{2,0,1:T(8,128)(2,1)S(1)}, u32[]{:S(2)}, u32[]{:S(2)}) async-start(bf16[8,16,768]{2,0,1:T(8,128)(2,1)} %reshape.116), calls=%async_computation.4 | async-start | bytes 393216 | tf_op jit(solution)/shard_map/all_to_all | solution.py:96
  175.9 9.6 %all-to-all-start.5 = ((bf16[8,16,768]{2,0,1:T(8,128)(2,1)}), bf16[8,16,768]{2,0,1:T(8,128)(2,1)S(1)}, u32[]{:S(2)}, u32[]{:S(2)}) async-start(bf16[8,16,768]{2,0,1:T(8,128)(2,1)} %reshape.117), calls=%async_computation.5 | async-start | bytes 393216 | tf_op jit(solution)/shard_map/all_to_all | solution.py:103
  185.5 9.6 %all-to-all-start.6 = ((bf16[8,16,768]{2,0,1:T(8,128)(2,1)}), bf16[8,16,768]{2,0,1:T(8,128)(2,1)S(1)}, u32[]{:S(2)}, u32[]{:S(2)}) async-start(bf16[8,16,768]{2,0,1:T(8,128)(2,1)} %reshape.118), calls=%async_computation.6 | async-start | bytes 393216 | tf_op jit(solution)/shard_map/all_to_all | solution.py:110
where the time goes:
time: 197 us; the launch traced here: 196 us
  blocking collectives  84.5 us (43%)
  starting transfers between devices  41.6 us (21%)
  waiting for transfers between devices  41.6 us (21%)
  local copies, waits for them, and re-layouts  19.9 us (10%)
  matrix products  5.4 us (3%)
    psum x1, blocking collectives, local(): scores, prob_grad = lax.psum((score_part, prob_part), ('col', 'seq'))  64.1 us
    all_to_all x1, blocking collectives, local(): lax.all_to_all(row_value, 'col', split_axis=0, concat_axis=1, tiled=True)  12.7 us
    unnamed x18, local copies, waits for them, and re-layouts  8.05 us
    all_to_all x1, blocking collectives, local(): lax.all_to_all(col_query.reshape(seq_dev, flat_width), 'seq', split_axis=...  7.69 us
    all_to_all x1, waiting for transfers between devices, local(): lax.all_to_all(row_key, 'col', split_axis=0, concat_axis=1, tiled=True)  5.42 us
    all_to_all x1, waiting for transfers between devices, local(): lax.all_to_all(query_grad.astype(jnp.bfloat16).reshape(own_rows, cols, wi...  5.29 us
    all_to_all x1, waiting for transfers between devices, local(): lax.all_to_all(col_value.reshape(seq_dev, flat_width), 'seq', split_axis=...  5.25 us
    all_to_all x1, waiting for transfers between devices, local(): lax.all_to_all(col_key.reshape(seq_dev, flat_width), 'seq', split_axis=1,...  4.63 us
  transfers between devices with their start and end apart: 12, of which 10 were waited for; matrix products, arithmetic and copies ran while one was open for 11% of the time, Pallas kernels for 0%

commit v1 on v0

--- a/solution.py
+++ b/solution.py
@@ -78,7 +78,7 @@
     prob_part = jnp.einsum(
         "sihe,sjhe->hij", gradient_row_block, value_row_block, preferred_element_type=jnp.float32
     )
-    scores, prob_grad = lax.psum((score_part, prob_part), ("col", "seq"))
+    scores, prob_grad = lax.psum(lax.psum((score_part, prob_part), "seq"), "col")
     attention_weight_rows, score_gradient_part = tied_terms(scores, prob_grad, row_scale)
     query_grad = jnp.einsum(
         "hij,sjhe->sihe", score_gradient_part, key_row_block, preferred_element_type=jnp.float32

time: 197 us -> 170 us (0.86)
  blocking collectives: 84.5 us -> 56.7 us
    psum x1 -> x2, blocking collectives: 64.1 us -> 36.3 us  [the longest x1 22.4 us: local(): lax.psum(lax.psum((score_part, prob_part), 'seq'), 'col')]
    unnamed x18 -> x22, local copies, waits for them, and re-layouts: 8.05 us -> 8.06 us
  transfers between devices with their start and end apart: 12 -> 12, of which waited for: 10 -> 10; matrix products, arithmetic and copies ran while one was open for 11% -> 13% of each run, Pallas kernels for 0% -> 0%
where the time goes in v1:
time: 170 us; the launch traced here: 168 us
  blocking collectives  56.7 us (33%)
  starting transfers between devices  41.6 us (24%)
  waiting for transfers between devices  41.6 us (24%)
  local copies, waits for them, and re-layouts  19.9 us (12%)
  matrix products  5.4 us (3%)
  other arithmetic  1.93 us (1%)
    psum x1, blocking collectives, local(): lax.psum(lax.psum((score_part, prob_part), 'seq'), 'col')  22.4 us
    psum x1, blocking collectives, local(): lax.psum((score_part, prob_part), 'seq')  13.9 us
    all_to_all x1, blocking collectives, local(): lax.all_to_all(row_query, 'col', split_axis=0, concat_axis=1, tiled=True)  12.7 us
    unnamed x22, local copies, waits for them, and re-layouts  8.06 us
    all_to_all x1, blocking collectives, local(): lax.all_to_all(col_value.reshape(seq_dev, flat_width), 'seq', split_axis=...  7.69 us
    all_to_all x1, waiting for transfers between devices, local(): lax.all_to_all(row_grad, 'col', split_axis=0, concat_axis=1, tiled=True)  5.42 us
    all_to_all x1, waiting for transfers between devices, local(): lax.all_to_all(key_gradient_part.astype(jnp.bfloat16).reshape(own_rows, c...  5.36 us
    all_to_all x1, waiting for transfers between devices, local(): lax.all_to_all(col_grad.reshape(seq_dev, flat_width), 'seq', split_axis=1...  5.25 us
  transfers between devices with their start and end apart: 12, of which 10 were waited for; matrix products, arithmetic and copies ran while one was open for 13% of the time, Pallas kernels for 0%

profile of v1, /device:TPU:0, one launch (start us, length us, event | category | flops | bytes accessed | tf_op | source)
XLA Modules:
  0.0 168.2 jit_solution(10150848662730892218)
XLA Ops:
  0.6 1.6 copy.132
  2.3 4.3 %all-to-all-start.7 = ((bf16[32,4,768]{2,0,1:T(8,128)(2,1)}), bf16[32,4,768]{2,0,1:T(8,128)(2,1)S(1)}, u32[]{:S(2)}, u32[]{:S(2)}) async-start(bf16[32,4,768]{2,0,1:T(8,128)(2,1)} %copy.132), calls=%async_computation.7 | async-start | bytes 393216 | tf_op jit(solution)/shard_map/all_to_all | solution.py:120
  6.6 0.7 copy.133
  7.3 4.6 %all-to-all-done.7 = bf16[32,4,768]{2,0,1:T(8,128)(2,1)S(1)} async-done(((bf16[32,4,768]{2,0,1:T(8,128)(2,1)}), bf16[32,4,768]{2,0,1:T(8,128)(2,1)S(1)}, u32[]{:S(2)}, u32[]{:S(2)}) %all-to-all-start.7) | async-done | bytes 196640 | tf_op jit(solution)/shard_map/all_to_all | solution.py:120
  11.9 3.4 %all-to-all-start.8 = ((bf16[32,4,768]{2,0,1:T(8,128)(2,1)}), bf16[32,4,768]{2,0,1:T(8,128)(2,1)S(1)}, u32[]{:S(2)}, u32[]{:S(2)}) async-start(bf16[32,4,768]{2,0,1:T(8,128)(2,1)} %copy.133), calls=%async_computation.8 | async-start | bytes 393216 | tf_op jit(solution)/shard_map/all_to_all | solution.py:123
  15.3 0.7 copy.136
  16.0 4.6 %all-to-all-done.8 = bf16[32,4,768]{2,0,1:T(8,128)(2,1)S(1)} async-done(((bf16[32,4,768]{2,0,1:T(8,128)(2,1)}), bf16[32,4,768]{2,0,1:T(8,128)(2,1)S(1)}, u32[]{:S(2)}, u32[]{:S(2)}) %all-to-all-start.8) | async-done | bytes 196640 | tf_op jit(solution)/shard_map/all_to_all | solution.py:123
  20.6 3.4 %all-to-all-start.9 = ((bf16[32,4,768]{2,0,1:T(8,128)(2,1)}), bf16[32,4,768]{2,0,1:T(8,128)(2,1)S(1)}, u32[]{:S(2)}, u32[]{:S(2)}) async-start(bf16[32,4,768]{2,0,1:T(8,128)(2,1)} %copy.136), calls=%async_computation.9 | async-start | bytes 393216 | tf_op jit(solution)/shard_map/all_to_all | solution.py:129
  24.0 5.2 %all-to-all-done.9 = bf16[32,4,768]{2,0,1:T(8,128)(2,1)S(1)} async-done(((bf16[32,4,768]{2,0,1:T(8,128)(2,1)}), bf16[32,4,768]{2,0,1:T(8,128)(2,1)S(1)}, u32[]{:S(2)}, u32[]{:S(2)}) %all-to-all-start.9) | async-done | bytes 196640 | tf_op jit(solution)/shard_map/all_to_all | solution.py:129
  29.3 7.7 %all_to_all.214 = bf16[32,4,768]{2,0,1:T(8,128)(2,1)S(1)} all-to-all(bf16[32,4,768]{2,0,1:T(8,128)(2,1)S(1)} %copy.137), channel_id=1, replica_groups=mesh['grp'=2,'col'=4,'seq'=4] {'seq'}, dimensions={1} | all-to-all | bytes 393216 | tf_op jit(solution)/shard_map/all_to_all | solution.py:126
  37.0 12.7 %all_to_all.215 = bf16[32,4,768]{2,1,0:T(4,128)(2,1)S(1)} all-to-all(bf16[32,4,768]{2,1,0:T(4,128)(2,1)S(1)} %copy-done.3), channel_id=1, replica_groups=mesh['grp'=2,'col'=4,'seq'=4] {'col'}, dimensions={0} | all-to-all | bytes 393216 | tf_op jit(solution)/shard_map/all_to_all | solution.py:61
  49.7 3.4 %all-to-all-start.1 = ((bf16[32,4,768]{2,1,0:T(4,128)(2,1)}), bf16[32,4,768]{2,1,0:T(4,128)(2,1)S(1)}, u32[]{:S(2)}, u32[]{:S(2)}) async-start(bf16[32,4,768]{2,1,0:T(4,128)(2,1)} %param.9), calls=%async_computation.1 | async-start | bytes 393216 | tf_op jit(solution)/shard_map/all_to_all | solution.py:62
  53.1 0.3 reshape.107
  53.4 0.4 copy.134
  53.8 0.3 reshape.108
  54.1 0.4 copy.135
  54.5 0.3 reshape.109
  54.8 0.4 copy.138
  55.2 0.3 reshape.110
  55.8 3.5 %all-to-all-done.1 = bf16[32,4,768]{2,1,0:T(4,128)(2,1)S(1)} async-done(((bf16[32,4,768]{2,1,0:T(4,128)(2,1)}), bf16[32,4,768]{2,1,0:T(4,128)(2,1)S(1)}, u32[]{:S(2)}, u32[]{:S(2)}) %all-to-all-start.1) | async-done | bytes 196640 | tf_op jit(solution)/shard_map/all_to_all | solution.py:62
  59.4 3.4 %all-to-all-start.2 = ((bf16[32,4,768]{2,1,0:T(4,128)(2,1)}), bf16[32,4,768]{2,1,0:T(4,128)(2,1)S(1)}, u32[]{:S(2)}, u32[]{:S(2)}) async-start(bf16[32,4,768]{2,1,0:T(4,128)(2,1)} %param.11), calls=%async_computation.2 | async-start | bytes 393216 | tf_op jit(solution)/shard_map/all_to_all | solution.py:64
  62.7 0.4 fusion.59
  63.2 0.3 fusion.15
  63.5 5.4 %all-to-all-done.2 = bf16[32,4,768]{2,1,0:T(4,128)(2,1)S(1)} async-done(((bf16[32,4,768]{2,1,0:T(4,128)(2,1)}), bf16[32,4,768]{2,1,0:T(4,128)(2,1)S(1)}, u32[]{:S(2)}, u32[]{:S(2)}) %all-to-all-start.2) | async-done | bytes 196640 | tf_op jit(solution)/shard_map/all_to_all | solution.py:64
  68.9 3.4 %all-to-all-start.3 = ((bf16[32,4,768]{2,1,0:T(4,128)(2,1)}), bf16[32,4,768]{2,1,0:T(4,128)(2,1)S(1)}, u32[]{:S(2)}, u32[]{:S(2)}) async-start(bf16[32,4,768]{2,1,0:T(4,128)(2,1)} %param.10), calls=%async_computation.3 | async-start | bytes 393216 | tf_op jit(solution)/shard_map/all_to_all | solution.py:63
  72.3 0.4 fusion.13
  72.7 0.4 copy.142
  73.1 1.0 all_to_all.191
  74.1 0.4 copy.145
  74.6 1.0 all_to_all.194
  75.5 0.6 fusion.14
  76.2 0.4 copy.148
  76.6 1.0 all_to_all.197
  77.6 0.3 reshape.100
  78.0 0.3 reshape.101
  78.4 0.3 reshape.102
  78.7 3.4 %all-to-all-start.11 = ((bf16[4,32,768]{2,1,0:T(8,128)(2,1)}), bf16[4,32,768]{2,1,0:T(8,128)(2,1)S(1)}, u32[]{:S(2)}, u32[]{:S(2)}) async-start(bf16[4,32,768]{2,1,0:T(8,128)(2,1)} %all_to_all.191), calls=%async_computation.11 | async-start | bytes 393216 | tf_op jit(solution)/shard_map/all_to_all | solution.py:142
  82.5 0.5 fusion.21
  83.0 0.5 convolution_bitcast_fusion
  83.5 13.9 %all-reduce = (f32[12,16,16]{2,1,0:T(8,128)S(1)}, f32[12,16,16]{2,1,0:T(8,128)S(1)}) all-reduce(f32[12,16,16]{2,1,0:T(8,128)S(1)} %convolution_bitcast_fusion, f32[12,16,16]{2,1,0:T(8,128)S(1)} %fusion.21), channel_id=1, replica_groups=mesh['grp'=2,'col'=4,'seq'=4] {'seq'}, use_global_device_ids=true, to_apply=%region_4.0 | all-reduce | flops 6144 | bytes 49152 | tf_op jit(solution)/shard_map/psum | solution.py:81
  97.4 22.4 %all-reduce.1 = (f32[12,16,16]{2,1,0:T(8,128)S(1)}, f32[12,16,16]{2,1,0:T(8,128)S(1)}) all-reduce(f32[12,16,16]{2,1,0:T(8,128)S(1)} %get-tuple-element.24, f32[12,16,16]{2,1,0:T(8,128)S(1)} %get-tuple-element.25), channel_id=1, replica_groups=mesh['grp'=2,'col'=4,'seq'=4] {'col'}, use_global_device_ids=true, to_apply=%region_5.0 | all-reduce | flops 6144 | bytes 49152 | tf_op jit(solution)/shard_map/psum | solution.py:81
  119.9 3.4 %all-to-all-start.12 = ((bf16[4,32,768]{2,1,0:T(8,128)(2,1)}), bf16[4,32,768]{2,1,0:T(8,128)(2,1)S(1)}, u32[]{:S(2)}, u32[]{:S(2)}) async-start(bf16[4,32,768]{2,1,0:T(8,128)(2,1)} %all_to_all.194), calls=%async_computation.12 | async-start | bytes 393216 | tf_op jit(solution)/shard_map/all_to_all | solution.py:145
  123.3 1.9 %fusion.58 = (f32[12,16]{1,0:T(8,128)S(1)}, f32[12,16,16]{2,1,0:T(8,128)S(1)}) fusion(f32[12,16,16]{2,1,0:T(8,128)S(1)} %get-tuple-element.27), kind=kOutput, calls=%fused_computation.74 | output fusion | flops 6159 | bytes 25344 | tf_op jit(solution)/shard_map/sub | solution.py:11
  125.2 3.4 %all-to-all-done.12 = bf16[4,32,768]{2,1,0:T(8,128)(2,1)S(1)} async-done(((bf16[4,32,768]{2,1,0:T(8,128)(2,1)}), bf16[4,32,768]{2,1,0:T(8,128)(2,1)S(1)}, u32[]{:S(2)}, u32[]{:S(2)}) %all-to-all-start.12) | async-done | bytes 196640 | tf_op jit(solution)/shard_map/all_to_all | solution.py:145
  128.6 3.4 %all-to-all-start.13 = ((bf16[4,32,768]{2,1,0:T(8,128)(2,1)}), bf16[4,32,768]{2,1,0:T(8,128)(2,1)S(1)}, u32[]{:S(2)}, u32[]{:S(2)}) async-start(bf16[4,32,768]{2,1,0:T(8,128)(2,1)} %all_to_all.197), calls=%async_computation.13 | async-start | bytes 393216 | tf_op jit(solution)/shard_map/all_to_all | solution.py:148
  131.9 0.8 fusion.11
  133.1 1.0 reshape.117
  134.0 3.2 %all-to-all-done.13 = bf16[4,32,768]{2,1,0:T(8,128)(2,1)S(1)} async-done(((bf16[4,32,768]{2,1,0:T(8,128)(2,1)}), bf16[4,32,768]{2,1,0:T(8,128)(2,1)S(1)}, u32[]{:S(2)}, u32[]{:S(2)}) %all-to-all-start.13) | async-done | bytes 196640 | tf_op jit(solution)/shard_map/all_to_all | solution.py:148
  137.2 3.5 %all-to-all-start.5 = ((bf16[8,16,768]{2,0,1:T(8,128)(2,1)}), bf16[8,16,768]{2,0,1:T(8,128)(2,1)S(1)}, u32[]{:S(2)}, u32[]{:S(2)}) async-start(bf16[8,16,768]{2,0,1:T(8,128)(2,1)} %reshape.117), calls=%async_computation.5 | async-start | bytes 393216 | tf_op jit(solution)/shard_map/all_to_all | solution.py:103
  140.8 0.7 fusion.10
  141.8 1.0 reshape.116
  142.8 5.4 %all-to-all-done.5 = bf16[8,16,768]{2,0,1:T(8,128)(2,1)S(1)} async-done(((bf16[8,16,768]{2,0,1:T(8,128)(2,1)}), bf16[8,16,768]{2,0,1:T(8,128)(2,1)S(1)}, u32[]{:S(2)}, u32[]{:S(2)}) %all-to-all-start.5) | async-done | bytes 196640 | tf_op jit(solution)/shard_map/all_to_all | solution.py:103
  148.2 3.4 %all-to-all-start.4 = ((bf16[8,16,768]{2,0,1:T(8,128)(2,1)}), bf16[8,16,768]{2,0,1:T(8,128)(2,1)S(1)}, u32[]{:S(2)}, u32[]{:S(2)}) async-start(bf16[8,16,768]{2,0,1:T(8,128)(2,1)} %reshape.116), calls=%async_computation.4 | async-start | bytes 393216 | tf_op jit(solution)/shard_map/all_to_all | solution.py:96
  151.5 0.7 fusion.12
  152.5 1.0 reshape.118
  153.5 4.2 %all-to-all-done.4 = bf16[8,16,768]{2,0,1:T(8,128)(2,1)S(1)} async-done(((bf16[8,16,768]{2,0,1:T(8,128)(2,1)}), bf16[8,16,768]{2,0,1:T(8,128)(2,1)S(1)}, u32[]{:S(2)}, u32[]{:S(2)}) %all-to-all-start.4) | async-done | bytes 196640 | tf_op jit(solution)/shard_map/all_to_all | solution.py:96
  157.8 3.4 %all-to-all-start.6 = ((bf16[8,16,768]{2,0,1:T(8,128)(2,1)}), bf16[8,16,768]{2,0,1:T(8,128)(2,1)S(1)}, u32[]{:S(2)}, u32[]{:S(2)}) async-start(bf16[8,16,768]{2,0,1:T(8,128)(2,1)} %reshape.118), calls=%async_computation.6 | async-start | bytes 393216 | tf_op jit(solution)/shard_map/all_to_all | solution.py:110
  161.1 0.8 copy.152
  162.0 0.8 copy.153
  162.8 0.8 copy.154
  163.6 0.8 copy.150
  164.5 0.8 copy.149
  165.3 2.0 %all-to-all-done.6 = bf16[8,16,768]{2,0,1:T(8,128)(2,1)S(1)} async-done(((bf16[8,16,768]{2,0,1:T(8,128)(2,1)}), bf16[8,16,768]{2,0,1:T(8,128)(2,1)S(1)}, u32[]{:S(2)}, u32[]{:S(2)}) %all-to-all-start.6) | async-done | bytes 196640 | tf_op jit(solution)/shard_map/all_to_all | solution.py:110
  167.4 0.8 copy.151
  (27 shorter events, 1.6 us)
Async XLA Ops:
  2.3 4.3 %copy-start = (bf16[32,4,768]{2,1,0:T(4,128)(2,1)S(1)}, bf16[32,4,768]{2,1,0:T(4,128)(2,1)}, u32[]{:S(2)}) copy-start(bf16[32,4,768]{2,1,0:T(4,128)(2,1)} %param.13) | copy-start | bytes 589828
  2.3 9.7 %all-to-all-start.7 = ((bf16[32,4,768]{2,0,1:T(8,128)(2,1)}), bf16[32,4,768]{2,0,1:T(8,128)(2,1)S(1)}, u32[]{:S(2)}, u32[]{:S(2)}) async-start(bf16[32,4,768]{2,0,1:T(8,128)(2,1)} %copy.132), calls=%async_computation.7 | async-start | bytes 393216 | tf_op jit(solution)/shard_map/all_to_all | solution.py:120
  7.3 8.0 %copy-start.1 = (bf16[32,4,768]{2,1,0:T(4,128)(2,1)S(1)}, bf16[32,4,768]{2,1,0:T(4,128)(2,1)}, u32[]{:S(2)}) copy-start(bf16[32,4,768]{2,1,0:T(4,128)(2,1)} %param.15) | copy-start | bytes 589828
  11.9 8.7 %all-to-all-start.8 = ((bf16[32,4,768]{2,0,1:T(8,128)(2,1)}), bf16[32,4,768]{2,0,1:T(8,128)(2,1)S(1)}, u32[]{:S(2)}, u32[]{:S(2)}) async-start(bf16[32,4,768]{2,0,1:T(8,128)(2,1)} %copy.133), calls=%async_computation.8 | async-start | bytes 393216 | tf_op jit(solution)/shard_map/all_to_all | solution.py:123
  16.0 8.0 %copy-start.2 = (bf16[32,4,768]{2,1,0:T(4,128)(2,1)S(1)}, bf16[32,4,768]{2,1,0:T(4,128)(2,1)}, u32[]{:S(2)}) copy-start(bf16[32,4,768]{2,1,0:T(4,128)(2,1)} %param.14) | copy-start | bytes 589828
  20.6 8.7 %all-to-all-start.9 = ((bf16[32,4,768]{2,0,1:T(8,128)(2,1)}), bf16[32,4,768]{2,0,1:T(8,128)(2,1)S(1)}, u32[]{:S(2)}, u32[]{:S(2)}) async-start(bf16[32,4,768]{2,0,1:T(8,128)(2,1)} %copy.136), calls=%async_computation.9 | async-start | bytes 393216 | tf_op jit(solution)/shard_map/all_to_all | solution.py:129
  24.0 13.0 %copy-start.3 = (bf16[32,4,768]{2,1,0:T(4,128)(2,1)S(1)}, bf16[32,4,768]{2,1,0:T(4,128)(2,1)}, u32[]{:S(2)}) copy-start(bf16[32,4,768]{2,1,0:T(4,128)(2,1)} %param.8) | copy-start | bytes 589828
  49.7 9.7 %all-to-all-start.1 = ((bf16[32,4,768]{2,1,0:T(4,128)(2,1)}), bf16[32,4,768]{2,1,0:T(4,128)(2,1)S(1)}, u32[]{:S(2)}, u32[]{:S(2)}) async-start(bf16[32,4,768]{2,1,0:T(4,128)(2,1)} %param.9), calls=%async_computation.1 | async-start | bytes 393216 | tf_op jit(solution)/shard_map/all_to_all | solution.py:62
  59.4 9.6 %all-to-all-start.2 = ((bf16[32,4,768]{2,1,0:T(4,128)(2,1)}), bf16[32,4,768]{2,1,0:T(4,128)(2,1)S(1)}, u32[]{:S(2)}, u32[]{:S(2)}) async-start(bf16[32,4,768]{2,1,0:T(4,128)(2,1)} %param.11), calls=%async_computation.2 | async-start | bytes 393216 | tf_op jit(solution)/shard_map/all_to_all | solution.py:64
  68.9 9.8 %all-to-all-start.3 = ((bf16[32,4,768]{2,1,0:T(4,128)(2,1)}), bf16[32,4,768]{2,1,0:T(4,128)(2,1)S(1)}, u32[]{:S(2)}, u32[]{:S(2)}) async-start(bf16[32,4,768]{2,1,0:T(4,128)(2,1)} %param.10), calls=%async_computation.3 | async-start | bytes 393216 | tf_op jit(solution)/shard_map/all_to_all | solution.py:63
  78.7 41.1 %all-to-all-start.11 = ((bf16[4,32,768]{2,1,0:T(8,128)(2,1)}), bf16[4,32,768]{2,1,0:T(8,128)(2,1)S(1)}, u32[]{:S(2)}, u32[]{:S(2)}) async-start(bf16[4,32,768]{2,1,0:T(8,128)(2,1)} %all_to_all.191), calls=%async_computation.11 | async-start | bytes 393216 | tf_op jit(solution)/shard_map/all_to_all | solution.py:142
  119.8 12.1 %copy-start.4 = (f32[12,16,16]{2,1,0:T(8,128)}, f32[12,16,16]{2,1,0:T(8,128)S(1)}, u32[]{:S(2)}) copy-start(f32[12,16,16]{2,1,0:T(8,128)S(1)} %get-tuple-element.26) | copy-start | bytes 36868
  119.9 8.7 %all-to-all-start.12 = ((bf16[4,32,768]{2,1,0:T(8,128)(2,1)}), bf16[4,32,768]{2,1,0:T(8,128)(2,1)S(1)}, u32[]{:S(2)}, u32[]{:S(2)}) async-start(bf16[4,32,768]{2,1,0:T(8,128)(2,1)} %all_to_all.194), calls=%async_computation.12 | async-start | bytes 393216 | tf_op jit(solution)/shard_map/all_to_all | solution.py:145
  128.6 8.7 %all-to-all-start.13 = ((bf16[4,32,768]{2,1,0:T(8,128)(2,1)}), bf16[4,32,768]{2,1,0:T(8,128)(2,1)S(1)}, u32[]{:S(2)}, u32[]{:S(2)}) async-start(bf16[4,32,768]{2,1,0:T(8,128)(2,1)} %all_to_all.197), calls=%async_computation.13 | async-start | bytes 393216 | tf_op jit(solution)/shard_map/all_to_all | solution.py:148
  134.0 6.8 %copy-start.5 = (f32[12,16,16]{2,1,0:T(8,128)S(1)}, f32[12,16,16]{2,1,0:T(8,128)}, u32[]{:S(2)}) copy-start(f32[12,16,16]{2,1,0:T(8,128)} %copy-done.4) | copy-start | bytes 36868
  137.2 10.9 %all-to-all-start.5 = ((bf16[8,16,768]{2,0,1:T(8,128)(2,1)}), bf16[8,16,768]{2,0,1:T(8,128)(2,1)S(1)}, u32[]{:S(2)}, u32[]{:S(2)}) async-start(bf16[8,16,768]{2,0,1:T(8,128)(2,1)} %reshape.117), calls=%async_computation.5 | async-start | bytes 393216 | tf_op jit(solution)/shard_map/all_to_all | solution.py:103
  148.2 9.6 %all-to-all-start.4 = ((bf16[8,16,768]{2,0,1:T(8,128)(2,1)}), bf16[8,16,768]{2,0,1:T(8,128)(2,1)S(1)}, u32[]{:S(2)}, u32[]{:S(2)}) async-start(bf16[8,16,768]{2,0,1:T(8,128)(2,1)} %reshape.116), calls=%async_computation.4 | async-start | bytes 393216 | tf_op jit(solution)/shard_map/all_to_all | solution.py:96
  157.8 9.6 %all-to-all-start.6 = ((bf16[8,16,768]{2,0,1:T(8,128)(2,1)}), bf16[8,16,768]{2,0,1:T(8,128)(2,1)S(1)}, u32[]{:S(2)}, u32[]{:S(2)}) async-start(bf16[8,16,768]{2,0,1:T(8,128)(2,1)} %reshape.118), calls=%async_computation.6 | async-start | bytes 393216 | tf_op jit(solution)/shard_map/all_to_all | solution.py:110
